TPU v7x, 128 devices: a whole 4x4x4 slice. The times are simulated.
128 devices in a mesh: seq: 16 (over z, x), head: 8 (over y, core).
Axes of the slice: x: 4, y: 4, z: 4, core: 2. Of those that a mesh axis runs over, the one named last changes fastest.
Arguments:
- x_inputs: bfloat16 [131072, 1024], P('seq', 'head'), may hold values from -6 to 6
- x_in_proj: bfloat16 [131072, 128], P('seq'), may hold values from -0.5 to 0.5
- x_out_proj: bfloat16 [131072, 128], P('seq'), may hold values from -6 to 6
- x_log_decay: float32 [16, 131072], P('head', 'seq'), may hold values from -0.6 to 0
- x_step: float32 [16, 131072], P('head', 'seq'), may hold values from 0 to 0.5
- z_source: int32 [131072], P('seq'), may hold values from 0 to 131071, as said below
- z_in_proj: bfloat16 [131072, 128], P('seq'), may hold values from -0.5 to 0.5
- z_out_proj: bfloat16 [131072, 128], P('seq'), may hold values from -6 to 6
- z_log_decay: float32 [16, 131072], P('head', 'seq'), may hold values from -0.6 to 0
- z_step: float32 [16, 131072], P('head', 'seq'), may hold values from 0 to 0.5
- gate_branch: bfloat16 [131072, 1024], P('seq', 'head'), may hold values from -8 to 8
- norm_gain: float32 [1024], P('head'), may hold values from 0.1 to 1.9
- out_weight: bfloat16 [1024, 512], P('head'), may hold values from -0.1875 to 0.1875
Outputs:
- layer_out: bfloat16 [131072, 512], P(('seq', 'head'))
Inputs may be any that keep to these rules, and one draw needn't show every extreme that they name: z_source is a permutation; every block of 8192 consecutive z-order positions takes exactly 512 tokens from each block of 8192 consecutive x-order tokens.
All inputs are finite; a program needn't handle non-finite values.
Results may differ from a plain program's by a relative error of at most 0.034.
Values may be sent and summed in bfloat16 or wider, within the bound.
No kernel may reach another device: no remote copies, remote signals or barrier semaphores. Data moves between devices by JAX's collectives and lax.ppermute only.
A program may use at most 128 MiB of HBM per device.

v0:
```python
import jax
import jax.numpy as jnp
from jax import lax
from jax.sharding import PartitionSpec as P

BLOCK = 512


def shifted(value, axis, steps):
    count = lax.axis_size(axis)
    initial, last = (max(0, -steps), min(count, count - steps))
    return lax.ppermute(value, axis, [(source, source + steps) for source in range(initial, last)])


def local_blocks(inputs, b_mat, c_mat, log_decay, step):
    count = inputs.shape[0]
    blocks = count // BLOCK
    heads = log_decay.shape[0]
    width = inputs.shape[1]
    head_width = width // heads
    state = b_mat.shape[1]
    cum = jnp.cumsum(log_decay.reshape(heads, blocks, BLOCK), axis=2).transpose(1, 0, 2)
    totals = cum[:, :, -1]
    step_blocks = step.reshape(heads, blocks, BLOCK).transpose(1, 0, 2)
    u_blocks = inputs.reshape(blocks, BLOCK, heads, head_width)
    b_blocks = b_mat.reshape(blocks, BLOCK, state)
    c_blocks = c_mat.reshape(blocks, BLOCK, state)
    rows = lax.broadcasted_iota(jnp.int32, (BLOCK, BLOCK), 0)
    cols = lax.broadcasted_iota(jnp.int32, (BLOCK, BLOCK), 1)
    lower = rows >= cols

    def one_block(carry, pieces):
        u_blk, b_blk, c_blk, cum_blk, d_blk, tot_blk = pieces
        scores = jnp.dot(c_blk, b_blk.T, preferred_element_type=jnp.float32)
        diff = jnp.where(lower[None], cum_blk[:, :, None] - cum_blk[:, None, :], -jnp.inf)
        weights = (scores[None] * jnp.exp(diff) * d_blk[:, None, :]).astype(jnp.bfloat16)
        intra = jnp.einsum("hts,shp->thp", weights, u_blk, preferred_element_type=jnp.float32)
        scale = (jnp.exp(tot_blk[:, None] - cum_blk) * d_blk).T
        contrib = (u_blk * scale[:, :, None]).astype(jnp.bfloat16)
        state_add = jnp.einsum("shp,sn->hpn", contrib, b_blk, preferred_element_type=jnp.float32)
        updated = jnp.exp(tot_blk)[:, None, None] * carry + state_add
        return (updated, (intra, carry))

    start = jnp.zeros((heads, head_width, state), jnp.float32)
    final, (intra_all, local_in) = lax.scan(
        one_block, start, (u_blocks, b_blocks, c_blocks, cum, step_blocks, totals)
    )
    return (intra_all, local_in, final, cum, totals, c_blocks)


def incoming_state(device_decay, final):

    def relay(index, pair):
        received = shifted(pair[1].astype(jnp.bfloat16), "seq", 1).astype(jnp.float32)
        return (received, device_decay[:, None, None] * received + final)

    start, _ = lax.fori_loop(0, lax.axis_size("seq") - 1, relay, (jnp.zeros_like(final), final))
    return start


def ssd_scan(inputs, b_mat, c_mat, log_decay, step):
    intra_all, local_in, final, cum, totals, c_blocks = local_blocks(
        inputs, b_mat, c_mat, log_decay, step
    )
    device_decay = jnp.exp(jnp.sum(totals, axis=0))
    start = incoming_state(device_decay, final)
    before = jnp.cumsum(totals, axis=0) - totals
    carried = local_in + jnp.exp(before)[:, :, None, None] * start[None]
    inter = jnp.einsum(
        "bqn,bhpn->bqhp", c_blocks, carried.astype(jnp.bfloat16), preferred_element_type=jnp.float32
    )
    inter = inter * jnp.exp(cum).transpose(0, 2, 1)[:, :, :, None]
    return (intra_all + inter).astype(jnp.bfloat16).reshape(inputs.shape)


def body(
    x_inputs,
    x_in_proj,
    x_out_proj,
    x_log_decay,
    x_step,
    z_source,
    z_in_proj,
    z_out_proj,
    z_log_decay,
    z_step,
    gate_branch,
    norm_gain,
    out_weight,
):
    y_x = ssd_scan(x_inputs, x_in_proj, x_out_proj, x_log_decay, x_step)
    whole = lax.all_gather(y_x, "seq", axis=0, tiled=True)
    u_z = jnp.take(whole, z_source, axis=0)
    y_z = ssd_scan(u_z, z_in_proj, z_out_proj, z_log_decay, z_step)
    gated = y_z.astype(jnp.float32) * jax.nn.silu(gate_branch.astype(jnp.float32))
    squares = lax.psum(jnp.sum(gated * gated, axis=1).astype(jnp.bfloat16), "head").astype(
        jnp.float32
    )
    mean_square = squares / (gated.shape[1] * lax.axis_size("head"))
    normed = (gated * lax.rsqrt(mean_square[:, None] + 1e-05) * norm_gain).astype(jnp.bfloat16)
    return lax.psum_scatter(
        jnp.dot(normed, out_weight, preferred_element_type=jnp.float32).astype(jnp.bfloat16),
        "head",
        scatter_dimension=0,
        tiled=True,
    )


def solution(mesh):
    placed = (
        P("seq", "head"),
        P("seq", None),
        P("seq", None),
        P("head", "seq"),
        P("head", "seq"),
        P("seq"),
        P("seq", None),
        P("seq", None),
        P("head", "seq"),
        P("head", "seq"),
        P("seq", "head"),
        P("head"),
        P("head", None),
    )
    return jax.shard_map(
        body, mesh=mesh, in_specs=placed, out_specs=P(("seq", "head"), None), check_vma=False
    )
```

profile of v0, /device:TPU:1, one launch (start us, length us, event | category | flops | bytes accessed | tf_op | source)
XLA Modules:
  0.0 932.3 jit_solution(13976984456812221220)
XLA Ops:
  14.1 8.2 reshape.159
  22.3 10.6 %copy.53 = bf16[16,512,2,64]{1,3,2,0:T(8,128)(2,1)} copy(bf16[16,512,2,64]{3,2,1,0:T(2,128)(2,1)} %reshape.159) | data formatting | bytes 4194304
  35.5 93.9 %while.56 = (s32[]{:T(128)}, f32[2,64,128]{2,1,0:T(8,128)S(1)}, f32[16,512,2,64]{1,3,2,0:T(8,128)}, f32[16,2,64,128]{3,2,1,0:T(8,128)S(1)}, f32[16,2]{1,0:T(8,12...) while((s32[]{:T(128)}, f32[2,64,128]{2,1,0:T(8,128)S(1)}, ...), condition=%wide.region_3.4_spmd.clone, body=%wide.region_2.3_spmd.clone.sunk | while | flops 154142720 | bytes 3853496 | solution.py:45
  130.2 101.2 %while.54 = (s32[]{:T(128)}, f32[2,64,128]{2,1,0:T(8,128)}, bf16[2,64,128]{2,1,0:T(8,128)(2,1)S(1)}, f32[2]{0:T(128)S(1)}, f32[2,64,128]{2,1,0:T(8,128)S(1)}, /*index=5*/s32[]{:T(128)}) while((s32[]{:T(128)}, f32[2,64,128]{2,1,0:T(8,128)}, bf16[2,64,128]{2,1,0:T(8,128)(2,1)S(1)}, f32[2]{0:T(128)S(1)}, f32[2,64,128]{2,1,0:T(8,128)S(1)}, ...), condition=%wide.region_7.8_spmd, body=%wide.region_6.7_spmd.sunk | while | flops 65538 | bytes 327797 | solution.py:57
  157.4 5.7 collective-permute-start
  164.8 5.7 collective-permute-start
  172.2 5.7 collective-permute-start
  179.6 5.9 collective-permute-start
  201.8 5.7 collective-permute-start
  216.6 5.7 collective-permute-start
  235.0 7.3 copy.73
  242.3 7.8 reshape.160
  254.2 221.1 %all-gather.2.cloned.1.call-done = bf16[131072,128]{1,0:T(8,128)(2,1)} async-done(((bf16[8192,128]{1,0:T(8,128)(2,1)}), bf16[131072,128]{1,0:T(8,128)(2,1)}) %all-gather.2.cloned.1.call-update) | async-done | bytes 33554448 | tf_op jit(solution)/shard_map/all_gather | solution.py:92
  475.3 122.0 %gather_fusion = bf16[8192,128]{1,0:T(8,128)(2,1)} fusion(bf16[131072,128]{1,0:T(8,128)(2,1)} %all-gather.2.cloned.1.call-done, s32[8192]{0:T(1024)S(1)} %fusion.69), kind=kCustom, calls=%fused_computation | custom fusion | bytes 4227072 | tf_op jit(solution)/shard_map/jit(_take)/gather | solution.py:93
  609.1 93.9 %while.57 = (s32[]{:T(128)}, f32[2,64,128]{2,1,0:T(8,128)S(1)}, f32[16,512,2,64]{1,3,2,0:T(8,128)}, f32[16,2,64,128]{3,2,1,0:T(8,128)S(1)}, f32[16,2]{1,0:T(8,12...) while((s32[]{:T(128)}, f32[2,64,128]{2,1,0:T(8,128)S(1)}, ...), condition=%wide.region_11.12_spmd.clone, body=%wide.region_10.11_spmd.clone.sunk | while | flops 154142720 | bytes 3853496 | solution.py:45
  703.7 99.8 %while.55 = (s32[]{:T(128)}, f32[2,64,128]{2,1,0:T(8,128)}, bf16[2,64,128]{2,1,0:T(8,128)(2,1)S(1)}, f32[2]{0:T(128)S(1)}, f32[2,64,128]{2,1,0:T(8,128)S(1)}, /*index=5*/s32[]{:T(128)}) while((s32[]{:T(128)}, f32[2,64,128]{2,1,0:T(8,128)}, bf16[2,64,128]{2,1,0:T(8,128)(2,1)S(1)}, f32[2]{0:T(128)S(1)}, f32[2,64,128]{2,1,0:T(8,128)S(1)}, ...), condition=%wide.region_15.16_spmd, body=%wide.region_14.15_spmd.sunk | while | flops 65538 | bytes 327797 | solution.py:57
  744.4 5.7 collective-permute-start.1
  751.8 5.9 collective-permute-start.1
  766.6 5.7 collective-permute-start.1
  781.3 5.7 collective-permute-start.1
  796.1 5.7 collective-permute-start.1
  816.4 36.8 %psum.7 = bf16[8192]{0:T(1024)(128)(2,1)S(1)} all-reduce(bf16[8192]{0:T(1024)(128)(2,1)S(1)} %multiply_reduce_fusion), channel_id=1, replica_groups=mesh['seq'=16,'head'=8] {'head'}, use_global_device_ids=true, to_apply=%region_17.18 | all-reduce | flops 8192 | bytes 32768 | tf_op jit(solution)/shard_map/psum | solution.py:96
  853.2 8.6 convolution_convert_fusion
  861.9 63.6 %reduce-scatter.2.cloned.1.call-done = bf16[1024,512]{1,0:T(8,128)(2,1)} async-done(((bf16[8192,512]{1,0:T(8,128)(2,1)}), bf16[1024,512]{1,0:T(8,128)(2,1)}) %reduce-scatter.2.cloned.1.call-update) | async-done | bytes 1048592 | tf_op jit(solution)/shard_map/reduce_scatter | solution.py:101
  (430 shorter events, 367.0 us)
Async XLA Ops:
  6.5 468.8 %all-gather.2.cloned.1.call-start = ((), (), s32[]{:S(2)}) async-start(), calls=%async_computation.1 | async-start | bytes 35651584 | tf_op jit(solution)/shard_map/all_gather | solution.py:92
  130.2 4.9 collective-permute-start
  151.6 5.2 collective-permute-start
  157.4 6.8 collective-permute-start
  164.8 6.8 collective-permute-start
  172.2 6.8 collective-permute-start
  179.6 6.9 collective-permute-start
  187.1 6.6 collective-permute-start
  194.4 6.8 collective-permute-start
  201.8 6.8 collective-permute-start
  209.2 6.8 collective-permute-start
  216.6 6.8 collective-permute-start
  224.0 6.8 collective-permute-start
  250.1 675.4 %reduce-scatter.2.cloned.1.call-start = ((), (), s32[]{:S(2)}) async-start(), calls=%async_computation.2 | async-start | bytes 9437184 | tf_op jit(solution)/shard_map/reduce_scatter | solution.py:101
  729.7 6.6 collective-permute-start.1
  737.0 6.8 collective-permute-start.1
  744.4 6.8 collective-permute-start.1
  751.8 6.9 collective-permute-start.1
  759.3 6.6 collective-permute-start.1
  766.6 6.8 collective-permute-start.1
  773.9 6.8 collective-permute-start.1
  781.3 6.8 collective-permute-start.1
  788.7 6.8 collective-permute-start.1
  796.1 6.8 collective-permute-start.1
  (12 other events, 924.5 us)
Sparse Core Ops, SparseCore 0:
  250.2 225.0 all-gather.1
  862.0 63.4 reduce-scatter.1
where the time goes:
time: 938 us; the launch traced here: 932 us
  waiting for transfers between devices  315 us (34%)
  local copies, waits for them, and re-layouts  186 us (20%)
  matrix products  173 us (18%)
  starting transfers between devices  152 us (16%)
  other arithmetic  53.4 us (6%)
  blocking collectives  36.8 us (4%)
  between operations  13.6 us (1%)
    all_gather x1, waiting for transfers between devices, body(): whole = lax.all_gather(y_x, 'seq', axis=0, tiled=True)  221 us
    ppermute x30, starting transfers between devices, shifted(): lax.ppermute(value, axis, [(source, source + steps) for source in range(i...  152 us
    gather x2, local copies, waits for them, and re-layouts, body(): u_z = jnp.take(whole, z_source, axis=0)  126 us
    dot_general x32, matrix products, one_block(): jnp.einsum('hts,shp->thp', weights, u_blk, preferred_element_type=jnp.flo...  80.4 us
    reduce_scatter x1, waiting for transfers between devices, body(): lax.psum_scatter(jnp.dot(normed, out_weight, preferred_element_type=jnp.f...  63.6 us
    dot_general x32, matrix products, one_block(): scores = jnp.dot(c_blk, b_blk.T, preferred_element_type=jnp.float32)  40.4 us
    psum x1, blocking collectives, body(): lax.psum(jnp.sum(gated * gated, axis=1).astype(jnp.bfloat16), 'head')  36.8 us
    dot_general x32, matrix products, one_block(): jnp.einsum('shp,sn->hpn', contrib, b_blk, preferred_element_type=jnp.floa...  36.7 us
  transfers between devices with their start and end apart: 32, of which 32 were waited for; matrix products, arithmetic and copies ran while one was open for 0% of the time, Pallas kernels for 0%

commit v1 on v0

--- a/solution.py
+++ b/solution.py
@@ -89,7 +89,9 @@
     out_weight,
 ):
     y_x = ssd_scan(x_inputs, x_in_proj, x_out_proj, x_log_decay, x_step)
-    whole = lax.all_gather(y_x, "seq", axis=0, tiled=True)
+    whole = jnp.concatenate(
+        lax.all_to_all(jnp.stack([y_x] * lax.axis_size("seq")), "seq", 0, 0), axis=0
+    )
     u_z = jnp.take(whole, z_source, axis=0)
     y_z = ssd_scan(u_z, z_in_proj, z_out_proj, z_log_decay, z_step)
     gated = y_z.astype(jnp.float32) * jax.nn.silu(gate_branch.astype(jnp.float32))

time: 938 us -> 1230 us (1.31)
  waiting for transfers between devices: 315 us -> 552 us
  starting transfers between devices: 152 us -> 174 us
  blocking collectives: 36.8 us -> 55.2 us
    all_to_all x0 -> x1, waiting for transfers between devices: none -> 457 us  [body(): lax.all_to_all(jnp.stack([y_x] * lax.axis_size('seq')), 'seq', 0, 0)]
    all_gather x1 -> x0, waiting for transfers between devices: 221 us -> none  [body(): whole = lax.all_gather(y_x, 'seq', axis=0, tiled=True)]
    another operation x11 -> x14, local copies, waits for them, and re-layouts: 7.51 us -> 32.8 us  [the longest x3 25.3 us: body(): jnp.stack([y_x] * lax.axis_size('seq'))]
    psum x1, blocking collectives: 36.8 us -> 55.2 us  [body(): lax.psum(jnp.sum(gated * gated, axis=1).astype(jnp.bfloat16), 'head')]
    all_to_all x0 -> x1, starting transfers between devices: none -> 16.3 us  [body(): lax.all_to_all(jnp.stack([y_x] * lax.axis_size('seq')), 'seq', 0, 0)]
    reshape x4 -> x2, local copies, waits for them, and re-layouts: 16 us -> 0.95 us  [the longest x2 15.1 us: ssd_scan(): return (intra_all + inter).astype(jnp.bfloat16).reshape(inputs.shape)]
where the time goes in v1:
time: 1230 us; the launch traced here: 1220 us
  waiting for transfers between devices  552 us (45%)
  local copies, waits for them, and re-layouts  196 us (16%)
  starting transfers between devices  174 us (14%)
  matrix products  173 us (14%)
  blocking collectives  55.2 us (4%)
  other arithmetic  53.4 us (4%)
  between operations  13.7 us (1%)
    all_to_all x1, waiting for transfers between devices, body(): lax.all_to_all(jnp.stack([y_x] * lax.axis_size('seq')), 'seq', 0, 0)  457 us
    ppermute x30, starting transfers between devices, shifted(): lax.ppermute(value, axis, [(source, source + steps) for source in range(i...  157 us
    gather x2, local copies, waits for them, and re-layouts, body(): u_z = jnp.take(whole, z_source, axis=0)  126 us
    dot_general x32, matrix products, one_block(): jnp.einsum('hts,shp->thp', weights, u_blk, preferred_element_type=jnp.flo...  80.4 us
    reduce_scatter x1, waiting for transfers between devices, body(): lax.psum_scatter(jnp.dot(normed, out_weight, preferred_element_type=jnp.f...  64.9 us
    psum x1, blocking collectives, body(): lax.psum(jnp.sum(gated * gated, axis=1).astype(jnp.bfloat16), 'head')  55.2 us
    dot_general x32, matrix products, one_block(): scores = jnp.dot(c_blk, b_blk.T, preferred_element_type=jnp.float32)  40.4 us
    dot_general x32, matrix products, one_block(): jnp.einsum('shp,sn->hpn', contrib, b_blk, preferred_element_type=jnp.floa...  36.7 us
  transfers between devices with their start and end apart: 32, of which 32 were waited for; matrix products, arithmetic and copies ran while one was open for 0% of the time, Pallas kernels for 0%

profile of v1, /device:TPU:1, one launch (start us, length us, event | category | flops | bytes accessed | tf_op | source)
XLA Modules:
  0.0 1220.0 jit_solution(9132744668073512003)
XLA Ops:
  14.1 8.2 reshape.161
  22.3 10.6 copy.53
  35.5 93.9 %while.56 = (s32[]{:T(128)}, f32[2,64,128]{2,1,0:T(8,128)S(1)}, f32[16,512,2,64]{1,3,2,0:T(8,128)}, f32[16,2,64,128]{3,2,1,0:T(8,128)S(1)}, f32[16,2]{1,0:T(8,12...) while((s32[]{:T(128)}, f32[2,64,128]{2,1,0:T(8,128)S(1)}, ...), condition=%wide.region_3.4_spmd.clone, body=%wide.region_2.3_spmd.clone.sunk | while | flops 154142720 | bytes 3853496 | solution.py:45
  130.1 101.2 %while.54 = (s32[]{:T(128)}, f32[2,64,128]{2,1,0:T(8,128)}, bf16[2,64,128]{2,1,0:T(8,128)(2,1)S(1)}, f32[2]{0:T(128)S(1)}, f32[2,64,128]{2,1,0:T(8,128)S(1)}, /*index=5*/s32[]{:T(128)}) while((s32[]{:T(128)}, f32[2,64,128]{2,1,0:T(8,128)}, bf16[2,64,128]{2,1,0:T(8,128)(2,1)S(1)}, f32[2]{0:T(128)S(1)}, f32[2,64,128]{2,1,0:T(8,128)S(1)}, ...), condition=%wide.region_7.8_spmd, body=%wide.region_6.7_spmd.sunk | while | flops 65538 | bytes 327797 | solution.py:57
  164.8 5.7 collective-permute-start
  179.6 5.9 collective-permute-start
  201.8 5.7 collective-permute-start
  216.6 5.7 collective-permute-start
  235.0 7.3 copy.73
  242.3 6.8 reshape.162
  249.0 11.2 stack.3
  260.2 16.3 %all-to-all-start = ((bf16[16,8192,128]{2,1,0:T(8,128)(2,1)}), bf16[16,8192,128]{2,1,0:T(8,128)(2,1)}, u32[]{:S(2)}, u32[]{:S(2)}) async-start(bf16[16,8192,128]{2,1,0:T(8,128)(2,1)} %stack.3), calls=%async_computation | async-start | bytes 67108864 | tf_op jit(solution)/shard_map/all_to_all | solution.py:93
  280.2 457.3 %all-to-all-done = bf16[16,8192,128]{2,1,0:T(8,128)(2,1)} async-done(((bf16[16,8192,128]{2,1,0:T(8,128)(2,1)}), bf16[16,8192,128]{2,1,0:T(8,128)(2,1)}, u32[]{:S(2)}, u32[]{:S(2)}) %all-to-all-start) | async-done | bytes 33554464 | tf_op jit(solution)/shard_map/all_to_all | solution.py:93
  737.6 122.0 %gather_fusion = bf16[8192,128]{1,0:T(8,128)(2,1)} fusion(bf16[131072,128]{1,0:T(8,128)(2,1)} %bitcast.10, s32[8192]{0:T(1024)S(1)} %fusion.69), kind=kCustom, calls=%fused_computation | custom fusion | bytes 4227072 | tf_op jit(solution)/shard_map/jit(_take)/gather | solution.py:95
  871.3 93.9 %while.57 = (s32[]{:T(128)}, f32[2,64,128]{2,1,0:T(8,128)S(1)}, f32[16,512,2,64]{1,3,2,0:T(8,128)}, f32[16,2,64,128]{3,2,1,0:T(8,128)S(1)}, f32[16,2]{1,0:T(8,12...) while((s32[]{:T(128)}, f32[2,64,128]{2,1,0:T(8,128)S(1)}, ...), condition=%wide.region_11.12_spmd.clone, body=%wide.region_10.11_spmd.clone.sunk | while | flops 154142720 | bytes 3853496 | solution.py:45
  965.9 105.6 %while.55 = (s32[]{:T(128)}, f32[2,64,128]{2,1,0:T(8,128)}, bf16[2,64,128]{2,1,0:T(8,128)(2,1)S(1)}, f32[2]{0:T(128)S(1)}, f32[2,64,128]{2,1,0:T(8,128)S(1)}, /*index=5*/s32[]{:T(128)}) while((s32[]{:T(128)}, f32[2,64,128]{2,1,0:T(8,128)}, bf16[2,64,128]{2,1,0:T(8,128)(2,1)S(1)}, f32[2]{0:T(128)S(1)}, f32[2,64,128]{2,1,0:T(8,128)S(1)}, ...), condition=%wide.region_15.16_spmd, body=%wide.region_14.15_spmd.sunk | while | flops 65538 | bytes 327797 | solution.py:57
  968.8 7.4 collective-permute-start.1
  997.6 5.7 collective-permute-start.1
  1012.4 5.9 collective-permute-start.1
  1027.1 5.7 collective-permute-start.1
  1034.5 5.7 collective-permute-start.1
  1084.4 55.2 %psum.7 = bf16[8192]{0:T(1024)(128)(2,1)S(1)} all-reduce(bf16[8192]{0:T(1024)(128)(2,1)S(1)} %multiply_reduce_fusion), channel_id=1, replica_groups=mesh['seq'=16,'head'=8] {'head'}, use_global_device_ids=true, to_apply=%region_17.18 | all-reduce | flops 8192 | bytes 32768 | tf_op jit(solution)/shard_map/psum | solution.py:98
  1139.6 8.6 convolution_convert_fusion
  1148.3 64.9 %reduce-scatter.2.cloned.1.call-done = bf16[1024,512]{1,0:T(8,128)(2,1)} async-done(((bf16[8192,512]{1,0:T(8,128)(2,1)}), bf16[1024,512]{1,0:T(8,128)(2,1)}) %reduce-scatter.2.cloned.1.call-update) | async-done | bytes 1048592 | tf_op jit(solution)/shard_map/reduce_scatter | solution.py:103
  (430 shorter events, 382.1 us)
Async XLA Ops:
  157.4 6.8 collective-permute-start
  164.8 6.8 collective-permute-start
  172.2 6.8 collective-permute-start
  179.6 6.9 collective-permute-start
  187.1 6.6 collective-permute-start
  194.4 6.8 collective-permute-start
  201.8 6.8 collective-permute-start
  209.2 6.8 collective-permute-start
  216.6 6.8 collective-permute-start
  224.0 6.8 collective-permute-start
  260.2 477.3 %all-to-all-start = ((bf16[16,8192,128]{2,1,0:T(8,128)(2,1)}), bf16[16,8192,128]{2,1,0:T(8,128)(2,1)}, u32[]{:S(2)}, u32[]{:S(2)}) async-start(bf16[16,8192,128]{2,1,0:T(8,128)(2,1)} %stack.3), calls=%async_computation | async-start | bytes 67108864 | tf_op jit(solution)/shard_map/all_to_all | solution.py:93
  276.6 936.6 %reduce-scatter.2.cloned.1.call-start = ((), (), s32[]{:S(2)}) async-start(), calls=%async_computation.2 | async-start | bytes 9437184 | tf_op jit(solution)/shard_map/reduce_scatter | solution.py:103
  968.8 8.4 collective-permute-start.1
  990.2 6.8 collective-permute-start.1
  997.6 6.8 collective-permute-start.1
  1005.0 6.8 collective-permute-start.1
  1012.4 6.9 collective-permute-start.1
  1019.9 6.6 collective-permute-start.1
  1027.1 6.8 collective-permute-start.1
  1034.5 6.8 collective-permute-start.1
  1041.9 6.8 collective-permute-start.1
  1049.3 6.8 collective-permute-start.1
  1056.7 6.8 collective-permute-start.1
  1064.1 6.8 collective-permute-start.1
  (12 other events, 1245.8 us)
Sparse Core Ops, SparseCore 0:
  1148.4 64.7 reduce-scatter.1
